TPU v7x, 128 devices: a whole 4x4x4 slice. The times are simulated.
128 devices in a mesh: ctx: 64 (over z_lo, x, y, core), fsdp: 2 (over z_hi).
Axes of the slice: x: 4, y: 4, z: 4 (z_hi: 2, z_lo: 2; z = z_hi * 2 + z_lo), core: 2. Of those that a mesh axis runs over, the one named last changes fastest.
Arguments:
- block_in: bfloat16 [2, 8192, 768], P('fsdp', 'ctx'), may hold values from -70 to 70
- out_grad: bfloat16 [2, 8192, 768], P('fsdp', 'ctx'), may hold values from -6 to 6
- ln1_gain: bfloat16 [768], P('fsdp'), may hold values from 0.5 to 1.5
- ln1_bias: bfloat16 [768], P('fsdp'), may hold values from -3 to 3
- w_qkv: bfloat16 [768, 2304], P('fsdp'), may hold values from -2 to 2
- q_bias: bfloat16 [768], P('fsdp'), may hold values from -3 to 3
- v_bias: bfloat16 [768], P('fsdp'), may hold values from -3 to 3
- w_proj: bfloat16 [768, 768], P('fsdp'), may hold values from -2 to 2
- b_proj: bfloat16 [768], P('fsdp'), may hold values from -3 to 3
- ln2_gain: bfloat16 [768], P('fsdp'), may hold values from 0.5 to 1.5
- ln2_bias: bfloat16 [768], P('fsdp'), may hold values from -3 to 3
- w_fc: bfloat16 [768, 3072], P('fsdp'), may hold values from -0.21875 to 0.21875
- b_fc: bfloat16 [3072], P('fsdp'), may hold values from -3 to 3
- w_out: bfloat16 [3072, 768], P('fsdp'), may hold values from -0.109375 to 0.109375
- b_out: bfloat16 [768], P('fsdp'), may hold values from -3 to 3
Outputs:
- block_out: bfloat16 [2, 8192, 768], P('fsdp', 'ctx')
- input_grad: float32 [2, 8192, 768], P('fsdp', 'ctx')
- grad_ln1_gain: float32 [768], P('fsdp')
- grad_ln1_bias: float32 [768], P('fsdp')
- grad_w_qkv: float32 [768, 2304], P('fsdp')
- grad_q_bias: float32 [768], P('fsdp')
- grad_v_bias: float32 [768], P('fsdp')
- grad_w_proj: float32 [768, 768], P('fsdp')
- grad_b_proj: float32 [768], P('fsdp')
- grad_ln2_gain: float32 [768], P('fsdp')
- grad_ln2_bias: float32 [768], P('fsdp')
- grad_w_fc: float32 [768, 3072], P('fsdp')
- grad_b_fc: float32 [3072], P('fsdp')
- grad_w_out: float32 [3072, 768], P('fsdp')
- grad_b_out: float32 [768], P('fsdp')
All inputs are finite; a program needn't handle non-finite values.
Results may differ from a plain program's by a relative error of at most 0.025.
The roundings to bfloat16 on the way count: a program that leaves them out, or rounds other values in their place, can miss the bound.
Values may be sent and summed in bfloat16 or wider, within the bound.
No kernel may reach another device: no remote copies, remote signals or barrier semaphores. Data moves between devices by JAX's collectives and lax.ppermute only.
A program may use at most 256 MiB of HBM per device.

v0:
```python
import math
import jax
import jax.numpy as jnp
from jax import lax
from jax.sharding import PartitionSpec as P

HEADS = 12
norm_epsilon = 1e-05
gelu_factor = 0.7978845608028654
gelu_cubic = 0.044715
masked_score = -1e30


def layer_norm(values, gain, offset):
    center = jnp.mean(values, axis=-1, keepdims=True)
    centered = values - center
    spread = jnp.mean(centered * centered, axis=-1, keepdims=True)
    return centered * lax.rsqrt(spread + norm_epsilon) * gain + offset


def gelu_tanh(values):
    return (
        0.5
        * values
        * (1.0 + jnp.tanh(gelu_factor * (values + gelu_cubic * values * values * values)))
    )


def score_grads(
    query_rows, grad_rows, lse_rows, delta_rows, key_rows, value_rows, allowed, score_scale
):
    scores = (
        jnp.einsum("thd,shd->hts", query_rows, key_rows, preferred_element_type=jnp.float32)
        * score_scale
    )
    scores = jnp.where(allowed[None], scores, masked_score)
    probabilities = jnp.where(allowed[None], jnp.exp(scores - lse_rows[:, :, None]), 0.0)
    grad_probs = jnp.einsum(
        "thd,shd->hts", grad_rows, value_rows, preferred_element_type=jnp.float32
    )
    grad_scores = (probabilities * (grad_probs - delta_rows[:, :, None]) * score_scale).astype(
        jnp.bfloat16
    )
    return (grad_scores, probabilities)


def body(
    block_in,
    out_grad,
    ln1_gain,
    ln1_bias,
    w_qkv,
    q_bias,
    v_bias,
    w_proj,
    b_proj,
    ln2_gain,
    ln2_bias,
    w_fc,
    b_fc,
    w_out,
    b_out,
):
    gathered = (
        lax.all_gather(ln1_gain, "fsdp", axis=0, tiled=True),
        lax.all_gather(ln1_bias, "fsdp", axis=0, tiled=True),
        lax.all_gather(w_qkv, "fsdp", axis=0, tiled=True),
        lax.all_gather(q_bias, "fsdp", axis=0, tiled=True),
        lax.all_gather(v_bias, "fsdp", axis=0, tiled=True),
        lax.all_gather(w_proj, "fsdp", axis=0, tiled=True),
        lax.all_gather(b_proj, "fsdp", axis=0, tiled=True),
        lax.all_gather(ln2_gain, "fsdp", axis=0, tiled=True),
        lax.all_gather(ln2_bias, "fsdp", axis=0, tiled=True),
        lax.all_gather(w_fc, "fsdp", axis=0, tiled=True),
        lax.all_gather(b_fc, "fsdp", axis=0, tiled=True),
        lax.all_gather(w_out, "fsdp", axis=0, tiled=True),
        lax.all_gather(b_out, "fsdp", axis=0, tiled=True),
    )
    gain_one = gathered[0].astype(jnp.float32)
    shift_one = gathered[1].astype(jnp.float32)
    qkv_weight = gathered[2]
    query_bias = gathered[3].astype(jnp.float32)
    value_bias = gathered[4].astype(jnp.float32)
    proj_weight = gathered[5]
    proj_bias = gathered[6].astype(jnp.float32)
    gain_two = gathered[7].astype(jnp.float32)
    shift_two = gathered[8].astype(jnp.float32)
    fc_weight = gathered[9]
    fc_bias = gathered[10].astype(jnp.float32)
    out_weight = gathered[11]
    out_bias = gathered[12].astype(jnp.float32)
    row_count = block_in.shape[1]
    width = block_in.shape[2]
    head_count = HEADS
    head_width = width // head_count
    score_scale = 1.0 / math.sqrt(head_width)
    row_total = row_count * lax.axis_size("ctx")
    first_query = lax.axis_index("ctx") * row_count
    query_pos = first_query + jnp.arange(row_count, dtype=jnp.int32)
    last_query = first_query + row_count - 1
    inputs_wide = block_in[0].astype(jnp.float32)
    normed_one = layer_norm(inputs_wide, gain_one, shift_one).astype(jnp.bfloat16)
    projected = jnp.dot(normed_one, qkv_weight, preferred_element_type=jnp.float32)
    queries = (projected[:, :width] + query_bias).astype(jnp.bfloat16)
    keys_local = projected[:, width : 2 * width].astype(jnp.bfloat16)
    values_local = (projected[:, 2 * width :] + value_bias).astype(jnp.bfloat16)
    query_heads = queries.reshape(row_count, head_count, head_width)
    initial = (
        jnp.full((head_count, row_count), masked_score, jnp.float32),
        jnp.zeros((head_count, row_count), jnp.float32),
        jnp.zeros((row_count, head_count, head_width), jnp.float32),
    )
    key_span = lax.all_gather(keys_local, "ctx", axis=0, tiled=True)
    value_span = lax.all_gather(values_local, "ctx", axis=0, tiled=True)
    span_total = key_span.shape[0]
    attend_span_rows = math.gcd(span_total, 512)

    def one_step(step_index, inner):
        offset = step_index * attend_span_rows
        key_rows = lax.dynamic_slice_in_dim(key_span, offset, attend_span_rows, 0).reshape(
            attend_span_rows, head_count, head_width
        )
        value_rows = lax.dynamic_slice_in_dim(value_span, offset, attend_span_rows, 0).reshape(
            attend_span_rows, head_count, head_width
        )

        def one_computed(state):
            maximum, denominator, accumulated = state
            key_pos = offset + jnp.arange(attend_span_rows, dtype=jnp.int32)
            allowed = key_pos[None, :] <= query_pos[:, None]
            scores = (
                jnp.einsum(
                    "thd,shd->hts", query_heads, key_rows, preferred_element_type=jnp.float32
                )
                * score_scale
            )
            scores = jnp.where(allowed[None], scores, masked_score)
            new_max = jnp.maximum(maximum, jnp.max(scores, axis=2))
            weights = jnp.where(allowed[None], jnp.exp(scores - new_max[:, :, None]), 0.0)
            factor = jnp.exp(maximum - new_max)
            denominator = denominator * factor + jnp.sum(weights, axis=2)
            accumulated = accumulated * jnp.transpose(factor)[:, :, None] + jnp.einsum(
                "hts,shd->thd",
                weights.astype(jnp.bfloat16),
                value_rows,
                preferred_element_type=jnp.float32,
            )
            return (new_max, denominator, accumulated)

        return lax.cond(offset > last_query, lambda state: state, one_computed, inner)

    maximum, denominator, accumulated = lax.fori_loop(
        0, span_total // attend_span_rows, one_step, initial
    )
    log_sums = maximum + jnp.log(denominator)
    attended = accumulated / jnp.transpose(denominator)[:, :, None]
    attn_rows = lax.optimization_barrier(attended.reshape(row_count, width).astype(jnp.bfloat16))
    residual_one = (
        jnp.dot(attn_rows, proj_weight, preferred_element_type=jnp.float32)
        + proj_bias
        + inputs_wide
    )
    normed_two = layer_norm(residual_one, gain_two, shift_two).astype(jnp.bfloat16)
    hidden_pre = jnp.dot(normed_two, fc_weight, preferred_element_type=jnp.float32) + fc_bias
    activated = gelu_tanh(hidden_pre).astype(jnp.bfloat16)
    output = (
        jnp.dot(activated, out_weight, preferred_element_type=jnp.float32) + out_bias + residual_one
    ).astype(jnp.bfloat16)
    cotangent = out_grad[0]
    grad_wide = cotangent.astype(jnp.float32)
    grad_out_weight = jnp.einsum(
        "tf,td->fd", activated, cotangent, preferred_element_type=jnp.float32
    )
    grad_out_bias = jnp.sum(grad_wide, axis=0)
    grad_activated = jnp.einsum(
        "td,fd->tf", cotangent, out_weight, preferred_element_type=jnp.float32
    )
    unused, gelu_back = jax.vjp(gelu_tanh, hidden_pre)
    grad_hidden = gelu_back(grad_activated)[0]
    grad_hidden_low = grad_hidden.astype(jnp.bfloat16)
    grad_fc_weight = jnp.einsum(
        "td,tf->df", normed_two, grad_hidden_low, preferred_element_type=jnp.float32
    )
    grad_fc_bias = jnp.sum(grad_hidden, axis=0)
    grad_normed_two = jnp.einsum(
        "tf,df->td", grad_hidden_low, fc_weight, preferred_element_type=jnp.float32
    )
    unused, norm_back_two = jax.vjp(layer_norm, residual_one, gain_two, shift_two)
    grad_residual, grad_gain_two, grad_shift_two = norm_back_two(grad_normed_two)
    grad_residual = grad_residual + grad_wide
    grad_residual_low = grad_residual.astype(jnp.bfloat16)
    grad_proj_weight = jnp.einsum(
        "td,te->de", attn_rows, grad_residual_low, preferred_element_type=jnp.float32
    )
    grad_proj_bias = jnp.sum(grad_residual, axis=0)
    grad_attn = lax.optimization_barrier(
        jnp.einsum(
            "te,de->td", grad_residual_low, proj_weight, preferred_element_type=jnp.float32
        ).astype(jnp.bfloat16)
    )
    grad_heads = grad_attn.reshape(row_count, head_count, head_width)
    delta_sums = jnp.transpose(
        jnp.sum(
            grad_heads.astype(jnp.float32)
            * attn_rows.reshape(row_count, head_count, head_width).astype(jnp.float32),
            axis=2,
        )
    )
    keys_all, values_all = (
        lax.all_gather(keys_local, "ctx", axis=0, tiled=True),
        lax.all_gather(values_local, "ctx", axis=0, tiled=True),
    )
    span_rows = math.gcd(row_total, 512)
    span_count = row_total // span_rows
    key_blocks = keys_all.reshape(span_count, span_rows, head_count, head_width)
    value_blocks = values_all.reshape(span_count, span_rows, head_count, head_width)
    zero_query = jnp.zeros((row_count, head_count, head_width), jnp.float32)

    def back_step(grad_query, inputs):
        key_rows, value_rows, step_index = inputs
        start_pos = step_index * span_rows

        def back_computed(running):
            key_pos = start_pos + jnp.arange(span_rows, dtype=jnp.int32)
            allowed = key_pos[None, :] <= query_pos[:, None]
            grad_scores, probabilities = score_grads(
                query_heads,
                grad_heads,
                log_sums,
                delta_sums,
                key_rows,
                value_rows,
                allowed,
                score_scale,
            )
            rounded = probabilities.astype(jnp.bfloat16)
            grad_key = jnp.einsum(
                "hts,thd->shd", grad_scores, query_heads, preferred_element_type=jnp.float32
            )
            grad_value = jnp.einsum(
                "hts,thd->shd", rounded, grad_heads, preferred_element_type=jnp.float32
            )
            updated = running + jnp.einsum(
                "hts,shd->thd", grad_scores, key_rows, preferred_element_type=jnp.float32
            )
            return (
                updated,
                jnp.concatenate(
                    [grad_key.reshape(span_rows, width), grad_value.reshape(span_rows, width)],
                    axis=1,
                ),
            )

        def skipped(running):
            return (running, jnp.zeros((span_rows, 2 * width), jnp.float32))

        return lax.cond(start_pos > last_query, skipped, back_computed, grad_query)

    grad_query, key_terms = lax.scan(
        back_step, zero_query, (key_blocks, value_blocks, jnp.arange(span_count, dtype=jnp.int32))
    )
    own_terms = lax.psum_scatter(
        key_terms.reshape(row_total, 2 * width), "ctx", scatter_dimension=0, tiled=True
    )
    grad_keys = own_terms[:, :width]
    grad_values = own_terms[:, width:]
    grad_query = grad_query.reshape(row_count, width)
    grad_query_bias = jnp.sum(grad_query, axis=0)
    grad_value_bias = jnp.sum(grad_values, axis=0)
    grad_projected = jnp.concatenate([grad_query, grad_keys, grad_values], axis=1).astype(
        jnp.bfloat16
    )
    grad_qkv_weight = jnp.einsum(
        "td,te->de", normed_one, grad_projected, preferred_element_type=jnp.float32
    )
    grad_normed_one = jnp.einsum(
        "te,de->td", grad_projected, qkv_weight, preferred_element_type=jnp.float32
    )
    unused, norm_back_one = jax.vjp(layer_norm, inputs_wide, gain_one, shift_one)
    grad_inputs, grad_gain_one, grad_shift_one = norm_back_one(grad_normed_one)
    grad_inputs = grad_inputs + grad_residual
    shards = (
        lax.psum_scatter(
            grad_gain_one.astype(jnp.bfloat16), "fsdp", scatter_dimension=0, tiled=True
        ).astype(jnp.float32),
        lax.psum_scatter(
            grad_shift_one.astype(jnp.bfloat16), "fsdp", scatter_dimension=0, tiled=True
        ).astype(jnp.float32),
        lax.psum_scatter(
            grad_qkv_weight.astype(jnp.bfloat16), "fsdp", scatter_dimension=0, tiled=True
        ).astype(jnp.float32),
        lax.psum_scatter(
            grad_query_bias.astype(jnp.bfloat16), "fsdp", scatter_dimension=0, tiled=True
        ).astype(jnp.float32),
        lax.psum_scatter(
            grad_value_bias.astype(jnp.bfloat16), "fsdp", scatter_dimension=0, tiled=True
        ).astype(jnp.float32),
        lax.psum_scatter(
            grad_proj_weight.astype(jnp.bfloat16), "fsdp", scatter_dimension=0, tiled=True
        ).astype(jnp.float32),
        lax.psum_scatter(
            grad_proj_bias.astype(jnp.bfloat16), "fsdp", scatter_dimension=0, tiled=True
        ).astype(jnp.float32),
        lax.psum_scatter(
            grad_gain_two.astype(jnp.bfloat16), "fsdp", scatter_dimension=0, tiled=True
        ).astype(jnp.float32),
        lax.psum_scatter(
            grad_shift_two.astype(jnp.bfloat16), "fsdp", scatter_dimension=0, tiled=True
        ).astype(jnp.float32),
        lax.psum_scatter(
            grad_fc_weight.astype(jnp.bfloat16), "fsdp", scatter_dimension=0, tiled=True
        ).astype(jnp.float32),
        lax.psum_scatter(
            grad_fc_bias.astype(jnp.bfloat16), "fsdp", scatter_dimension=0, tiled=True
        ).astype(jnp.float32),
        lax.psum_scatter(
            grad_out_weight.astype(jnp.bfloat16), "fsdp", scatter_dimension=0, tiled=True
        ).astype(jnp.float32),
        lax.psum_scatter(
            grad_out_bias.astype(jnp.bfloat16), "fsdp", scatter_dimension=0, tiled=True
        ).astype(jnp.float32),
    )
    totals = lax.psum(
        (
            shards[0],
            shards[1],
            shards[2],
            shards[3],
            shards[4],
            shards[5],
            shards[6],
            shards[7],
            shards[8],
            shards[9],
            shards[10],
            shards[11],
            shards[12],
        ),
        "ctx",
    )
    return (
        output[None],
        grad_inputs[None],
        totals[0],
        totals[1],
        totals[2],
        totals[3],
        totals[4],
        totals[5],
        totals[6],
        totals[7],
        totals[8],
        totals[9],
        totals[10],
        totals[11],
        totals[12],
    )


def solution(mesh):
    in_specs = (
        P("fsdp", "ctx", None),
        P("fsdp", "ctx", None),
        P("fsdp"),
        P("fsdp"),
        P("fsdp", None),
        P("fsdp"),
        P("fsdp"),
        P("fsdp", None),
        P("fsdp"),
        P("fsdp"),
        P("fsdp"),
        P("fsdp", None),
        P("fsdp"),
        P("fsdp", None),
        P("fsdp"),
    )
    out_specs = (
        P("fsdp", "ctx", None),
        P("fsdp", "ctx", None),
        P("fsdp"),
        P("fsdp"),
        P("fsdp", None),
        P("fsdp"),
        P("fsdp"),
        P("fsdp", None),
        P("fsdp"),
        P("fsdp"),
        P("fsdp"),
        P("fsdp", None),
        P("fsdp"),
        P("fsdp", None),
        P("fsdp"),
    )
    return jax.shard_map(body, mesh=mesh, in_specs=in_specs, out_specs=out_specs, check_vma=False)
```

profile of v0, /device:TPU:0, one launch (start us, length us, event | category | flops | bytes accessed | tf_op | source)
XLA Modules:
  0.0 1733.6 jit_solution(4564429500221950973)
XLA Ops:
  8.7 6.2 all-gather.1
  15.6 5.8 all-gather
  24.4 41.3 %all-gather.16.cloned.1.call-done = bf16[768,2304]{1,0:T(8,128)(2,1)} async-done(((bf16[384,2304]{1,0:T(8,128)(2,1)}), bf16[768,2304]{1,0:T(8,128)(2,1)}) %all-gather.16.cloned.1.call-update) | async-done | bytes 3538960 | tf_op jit(solution)/shard_map/all_gather | solution.py:67
  69.3 5.8 all-gather.3
  75.2 5.8 all-gather.2
  83.8 5.8 all-gather.4
  89.7 5.9 all-gather.7
  95.6 5.8 all-gather.6
  101.5 5.8 all-gather.5
  107.5 79.1 %all-gather.18.cloned.1.call-done = bf16[8192,768]{1,0:T(8,128)(2,1)} async-done(((bf16[128,768]{1,0:T(8,128)(2,1)}), bf16[8192,768]{1,0:T(8,128)(2,1)}) %all-gather.18.cloned.1.call-update) | async-done | bytes 12582928 | tf_op jit(solution)/shard_map/all_gather | solution.py:113
  186.6 16.3 copy.76
  203.0 103.3 %all-gather.20.cloned.1.call-done = bf16[8192,768]{1,0:T(8,128)(2,1)} async-done(((bf16[128,768]{1,0:T(8,128)(2,1)}), bf16[8192,768]{1,0:T(8,128)(2,1)}) %all-gather.20.cloned.1.call-update) | async-done | bytes 12582928 | tf_op jit(solution)/shard_map/all_gather | solution.py:114
  306.2 15.8 copy.77
  322.1 5.7 while.34
  322.2 4.4 conditional.6
  327.9 6.2 all-gather.22.cloned.1.call-done
  336.0 65.6 %all-gather.24.cloned.1.call-done = bf16[768,3072]{1,0:T(8,128)(2,1)} async-done(((bf16[384,3072]{1,0:T(8,128)(2,1)}), bf16[768,3072]{1,0:T(8,128)(2,1)}) %all-gather.24.cloned.1.call-update) | async-done | bytes 4718608 | tf_op jit(solution)/shard_map/all_gather | solution.py:74
  404.9 64.3 %all-gather.26.cloned.1.call-done = bf16[3072,768]{1,0:T(8,128)(2,1)} async-done(((bf16[1536,768]{1,0:T(8,128)(2,1)}), bf16[3072,768]{1,0:T(8,128)(2,1)}) %all-gather.26.cloned.1.call-update) | async-done | bytes 4718608 | tf_op jit(solution)/shard_map/all_gather | solution.py:76
  469.2 5.4 fusion.95
  477.3 9.5 copy.108
  486.9 18.8 %copy.81 = bf16[16,512,12,64]{1,3,2,0:T(8,128)(2,1)} copy(bf16[16,512,12,64]{1,0,3,2:T(8,128)(2,1)S(1)} %bitcast.175) | data formatting | bytes 25165824
  506.3 4.6 copy.109
  510.9 18.6 %copy.82 = bf16[16,512,12,64]{1,3,2,0:T(8,128)(2,1)} copy(bf16[16,512,12,64]{1,0,3,2:T(8,128)(2,1)S(1)} %bitcast.176) | data formatting | bytes 25165824
  532.7 134.6 %while.35 = (s32[]{:T(128)}, f32[128,12,64]{0,2,1:T(8,128)}, f32[16,512,1536]{2,1,0:T(8,128)}, s32[16]{0:T(128)S(1)}, s32[]{:T(128)}, /*index=5*/bf16[16,512,12,...) while((s32[]{:T(128)}, f32[128,12,64]{0,2,1:T(8,128)}, ...), condition=%wide.region_16.17_spmd.clone, body=%wide.region_13.16_spmd.clone.sunk | while | flops 514491008 | bytes 40333600 | solution.py:259
  533.9 10.1 conditional.7
  546.4 3.7 constant_dynamic-update-slice_fusion.2
  554.1 3.8 constant_dynamic-update-slice_fusion.2
  562.0 3.8 constant_dynamic-update-slice_fusion.2
  569.8 3.7 constant_dynamic-update-slice_fusion.2
  577.6 3.7 constant_dynamic-update-slice_fusion.2
  585.3 3.7 constant_dynamic-update-slice_fusion.2
  593.1 3.8 constant_dynamic-update-slice_fusion.2
  600.9 3.8 constant_dynamic-update-slice_fusion.2
  608.7 3.8 constant_dynamic-update-slice_fusion.2
  616.6 3.8 constant_dynamic-update-slice_fusion.2
  632.2 3.8 constant_dynamic-update-slice_fusion.2
  647.8 3.8 constant_dynamic-update-slice_fusion.2
  655.6 3.8 constant_dynamic-update-slice_fusion.2
  675.2 3.8 convolution_convert_fusion
  680.5 502.5 %reduce-scatter.6.cloned.1.call-done = f32[128,1536]{1,0:T(8,128)} async-done(((f32[8192,1536]{1,0:T(8,128)}), f32[128,1536]{1,0:T(8,128)}) %reduce-scatter.6.cloned.1.call-update) | async-done | bytes 786448 | tf_op jit(solution)/shard_map/reduce_scatter | solution.py:262
  1188.5 5.8 all-gather.8
  1198.1 4.1 fusion.55
  1202.3 7.9 reduce-scatter.10.cloned.1.call-done
  1210.2 66.5 %reduce-scatter.12.cloned.1.call-done = bf16[384,3072]{1,0:T(8,128)(2,1)} async-done(((bf16[768,3072]{1,0:T(8,128)(2,1)}), bf16[384,3072]{1,0:T(8,128)(2,1)}) %reduce-scatter.12.cloned.1.call-update) | async-done | bytes 2359312 | tf_op jit(solution)/shard_map/reduce_scatter | solution.py:310
  1276.7 66.2 %reduce-scatter.14.cloned.1.call-done = bf16[1536,768]{1,0:T(8,128)(2,1)} async-done(((bf16[3072,768]{1,0:T(8,128)(2,1)}), bf16[1536,768]{1,0:T(8,128)(2,1)}) %reduce-scatter.14.cloned.1.call-update) | async-done | bytes 2359312 | tf_op jit(solution)/shard_map/reduce_scatter | solution.py:316
  1348.1 8.4 all-reduce.10
  1356.9 40.2 %reduce-scatter.8.cloned.1.call-done = bf16[384,2304]{1,0:T(8,128)(2,1)} async-done(((bf16[768,2304]{1,0:T(8,128)(2,1)}), bf16[384,2304]{1,0:T(8,128)(2,1)}) %reduce-scatter.8.cloned.1.call-update) | async-done | bytes 1769488 | tf_op jit(solution)/shard_map/reduce_scatter | solution.py:289
  1397.1 330.0 %all-reduce.12 = (f32[384]{0:T(512)}, f32[384]{0:T(512)}, f32[384,2304]{1,0:T(8,128)}, f32[384]{0:T(512)}, f32[384]{0:T(512)}, /*index=5*/f32[384,768]{1,0:T(8,1...) all-reduce(f32[384]{0:T(512)S(1)} %get-tuple-element.680, ...), channel_id=1, replica_groups=mesh['ctx'=64,'fsdp'=2] {'ctx'}, use_global_device_ids=true, to_apply=%region_22.23 | all-reduce | flops 3543552 | bytes 21270528 | tf_op jit(solution)/shard_map/psum | solution.py:323
  (380 shorter events, 131.0 us)
Async XLA Ops:
  7.2 58.5 %all-gather.16.cloned.1.call-start = ((), (), s32[]{:S(2)}) async-start(), calls=%async_computation.5 | async-start | bytes 5308416 | tf_op jit(solution)/shard_map/all_gather | solution.py:67
  7.9 61.4 %copy-start.47 = (bf16[384]{0:T(512)(128)(2,1)S(1)}, bf16[384]{0:T(512)(128)(2,1)}, u32[]{:S(2)}) copy-start(bf16[384]{0:T(512)(128)(2,1)} %param.29) | copy-start | bytes 2308
  7.9 67.3 %copy-start.48 = (bf16[384]{0:T(512)(128)(2,1)S(1)}, bf16[384]{0:T(512)(128)(2,1)}, u32[]{:S(2)}) copy-start(bf16[384]{0:T(512)(128)(2,1)} %param.28) | copy-start | bytes 2308
  7.9 178.7 %all-gather.18.cloned.1.call-start = ((), (), s32[]{:S(2)}) async-start(), calls=%async_computation.6 | async-start | bytes 12779520 | tf_op jit(solution)/shard_map/all_gather | solution.py:113
  14.9 66.2 %copy-start.26 = (f32[768]{0:T(1024)}, f32[768]{0:T(1024)S(1)}, u32[]{:S(2)}) copy-start(f32[768]{0:T(1024)S(1)} %reshape.253) | copy-start | bytes 9220
  21.5 59.6 %copy-start.19 = (f32[768]{0:T(1024)}, f32[768]{0:T(1024)S(1)}, u32[]{:S(2)}) copy-start(f32[768]{0:T(1024)S(1)} %reshape.252) | copy-start | bytes 9220
  22.6 58.5 %copy-start.31 = (f32[128]{0:T(128)}, f32[128]{0:T(128)S(1)}, u32[]{:S(2)}) copy-start(f32[128]{0:T(128)S(1)} %broadcast_multiply_fusion.1) | copy-start | bytes 1540
  24.4 56.7 %copy-start.36 = (f32[128]{0:T(128)}, f32[128]{0:T(128)S(1)}, u32[]{:S(2)}) copy-start(f32[128]{0:T(128)S(1)} %fusion.82) | copy-start | bytes 1540
  69.3 237.0 %all-gather.20.cloned.1.call-start = ((), (), s32[]{:S(2)}) async-start(), calls=%async_computation.7 | async-start | bytes 12779520 | tf_op jit(solution)/shard_map/all_gather | solution.py:114
  81.1 8.5 copy-start.46
  81.2 14.4 copy-start.50
  81.2 20.3 %copy-start.51 = (bf16[384]{0:T(512)(128)(2,1)S(1)}, bf16[384]{0:T(512)(128)(2,1)}, u32[]{:S(2)}) copy-start(bf16[384]{0:T(512)(128)(2,1)} %param.32) | copy-start | bytes 2308
  81.9 252.1 %all-gather.22.cloned.1.call-start = ((), (), s32[]{:S(2)}) async-start(), calls=%async_computation.8 | async-start | bytes 1769472 | tf_op jit(solution)/shard_map/all_gather | solution.py:70
  82.5 319.1 %all-gather.24.cloned.1.call-start = ((), (), s32[]{:S(2)}) async-start(), calls=%async_computation.9 | async-start | bytes 7077888 | tf_op jit(solution)/shard_map/all_gather | solution.py:74
  83.1 386.1 %all-gather.26.cloned.1.call-start = ((), (), s32[]{:S(2)}) async-start(), calls=%async_computation.10 | async-start | bytes 7077888 | tf_op jit(solution)/shard_map/all_gather | solution.py:76
  83.7 1099.3 %reduce-scatter.6.cloned.1.call-start = ((), (), s32[]{:S(2)}) async-start(), calls=%async_computation.11 | async-start | bytes 51118080 | tf_op jit(solution)/shard_map/reduce_scatter | solution.py:262
  101.5 300.2 %copy-start.24 = (f32[768]{0:T(1024)}, f32[768]{0:T(1024)S(1)}, u32[]{:S(2)}) copy-start(f32[768]{0:T(1024)S(1)} %reshape.258) | copy-start | bytes 9220
  107.4 294.3 %copy-start.21 = (f32[768]{0:T(1024)}, f32[768]{0:T(1024)S(1)}, u32[]{:S(2)}) copy-start(f32[768]{0:T(1024)S(1)} %reshape.257) | copy-start | bytes 9220
  322.1 12.0 copy-start.5
  327.9 202.9 %copy-start.11 = (bf16[128,12,64]{0,2,1:T(8,128)(2,1)}, bf16[128,12,64]{0,2,1:T(8,128)(2,1)S(1)}, u32[]{:S(2)}) copy-start(bf16[128,12,64]{0,2,1:T(8,128)(2,1)S(1)} %divide_convert_fusion) | copy-start | bytes 589828
  335.8 141.2 %copy-start.1 = (f32[128,768]{1,0:T(8,128)}, f32[128,768]{1,0:T(8,128)S(1)}, u32[]{:S(2)}) copy-start(f32[128,768]{1,0:T(8,128)S(1)} %get-tuple-element.668) | copy-start | bytes 1179652
  335.8 69.1 %copy-start.28 = (f32[128]{0:T(128)}, f32[128]{0:T(128)S(1)}, u32[]{:S(2)}) copy-start(f32[128]{0:T(128)S(1)} %broadcast_multiply_fusion) | copy-start | bytes 1540
  336.0 68.9 %copy-start.55 = (f32[128]{0:T(128)}, f32[128]{0:T(128)S(1)}, u32[]{:S(2)}) copy-start(f32[128]{0:T(128)S(1)} %multiply_reduce_fusion.2) | copy-start | bytes 1540
  336.0 68.9 %copy-start.33 = (f32[128]{0:T(128)}, f32[128]{0:T(128)S(1)}, u32[]{:S(2)}) copy-start(f32[128]{0:T(128)S(1)} %fusion.83) | copy-start | bytes 1540
  401.6 67.6 %copy-start.8 = (bf16[1,128,768]{2,1,0:T(8,128)(2,1)S(1)}, bf16[1,128,768]{2,1,0:T(8,128)(2,1)}, u32[]{:S(2)}) copy-start(bf16[1,128,768]{2,1,0:T(8,128)(2,1)} %param.24) | copy-start | bytes 589828
  404.9 69.7 %copy-start.3 = (f32[128,3072]{1,0:T(8,128)}, f32[128,3072]{1,0:T(8,128)S(1)}, u32[]{:S(2)}) copy-start(f32[128,3072]{1,0:T(8,128)S(1)} %convolution_add_fusion) | copy-start | bytes 4718596
  469.2 5.4 copy-start.29
  469.2 5.4 copy-start.34
  477.3 52.2 %copy-start.6 = (f32[128,768]{1,0:T(8,128)}, f32[128,768]{1,0:T(8,128)S(1)}, u32[]{:S(2)}) copy-start(f32[128,768]{1,0:T(8,128)S(1)} %get-tuple-element.656) | copy-start | bytes 1179652
  477.3 52.2 %copy-start.43 = (f32[128]{0:T(128)}, f32[128]{0:T(128)S(1)}, u32[]{:S(2)}) copy-start(f32[128]{0:T(128)S(1)} %negate_multiply_fusion.1) | copy-start | bytes 1540
  486.8 19.4 %slice-start = ((s8[12582912]{0:T(1024)(128)(4,1)}), s8[4194304]{0:T(1024)(128)(4,1)S(1)}, s32[]{:S(2)}) async-start(s8[12582912]{0:T(1024)(128)(4,1)} %bitcast.169), calls=%async_computation.16 | async-start | bytes 8388608
  486.8 19.4 %slice-start.1 = ((s8[12582912]{0:T(1024)(128)(4,1)}), s8[4194304]{0:T(1024)(128)(4,1)S(1)}, s32[]{:S(2)}) async-start(s8[12582912]{0:T(1024)(128)(4,1)} %bitcast.169), calls=%async_computation.17 | async-start | bytes 8388608
  486.9 19.4 %slice-start.2 = ((s8[12582912]{0:T(1024)(128)(4,1)}), s8[4194304]{0:T(1024)(128)(4,1)S(1)}, s32[]{:S(2)}) async-start(s8[12582912]{0:T(1024)(128)(4,1)} %bitcast.169), calls=%async_computation.18 | async-start | bytes 8388608
  510.9 18.6 %copy-start.10 = (bf16[768,768]{1,0:T(8,128)(2,1)S(1)}, bf16[768,768]{1,0:T(8,128)(2,1)}, u32[]{:S(2)}) copy-start(bf16[768,768]{1,0:T(8,128)(2,1)} %all-gather.22.cloned.1.call-done) | copy-start | bytes 3538948
  667.3 542.8 %reduce-scatter.10.cloned.1.call-start = ((), (), s32[]{:S(2)}) async-start(), calls=%async_computation.13 | async-start | bytes 1769472 | tf_op jit(solution)/shard_map/reduce_scatter | solution.py:298
  669.9 606.8 %reduce-scatter.12.cloned.1.call-start = ((), (), s32[]{:S(2)}) async-start(), calls=%async_computation.14 | async-start | bytes 7077888 | tf_op jit(solution)/shard_map/reduce_scatter | solution.py:310
  673.8 669.2 %reduce-scatter.14.cloned.1.call-start = ((), (), s32[]{:S(2)}) async-start(), calls=%async_computation.15 | async-start | bytes 7077888 | tf_op jit(solution)/shard_map/reduce_scatter | solution.py:316
  679.0 505.2 %copy-start.20 = (f32[768]{0:T(1024)S(1)}, f32[768]{0:T(1024)}, u32[]{:S(2)}) copy-start(f32[768]{0:T(1024)} %copy-done.19) | copy-start | bytes 9220
  679.0 505.2 %copy-start.27 = (f32[768]{0:T(1024)S(1)}, f32[768]{0:T(1024)}, u32[]{:S(2)}) copy-start(f32[768]{0:T(1024)} %copy-done.26) | copy-start | bytes 9220
  679.0 505.2 %copy-start.32 = (f32[128]{0:T(128)S(1)}, f32[128]{0:T(128)}, u32[]{:S(2)}) copy-start(f32[128]{0:T(128)} %copy-done.31) | copy-start | bytes 1540
  679.0 718.1 %reduce-scatter.8.cloned.1.call-start = ((), (), s32[]{:S(2)}) async-start(), calls=%async_computation.12 | async-start | bytes 5308416 | tf_op jit(solution)/shard_map/reduce_scatter | solution.py:289
  680.5 507.3 %copy-start.17 = (bf16[128,768]{1,0:T(8,128)(2,1)}, bf16[128,768]{1,0:T(8,128)(2,1)S(1)}, u32[]{:S(2)}) copy-start(bf16[128,768]{1,0:T(8,128)(2,1)S(1)} %copy.84) | copy-start | bytes 589828
  1187.8 7.8 copy-start.57
  1198.1 144.8 %copy-start.15 = (f32[128,1536]{1,0:T(8,128)S(1)}, f32[128,1536]{1,0:T(8,128)}, u32[]{:S(2)}) copy-start(f32[128,1536]{1,0:T(8,128)} %reduce-scatter.6.cloned.1.call-done) | copy-start | bytes 2359300
  1202.3 144.4 %copy-start.54 = (f32[128]{0:T(128)S(1)}, f32[128]{0:T(128)}, u32[]{:S(2)}) copy-start(f32[128]{0:T(128)} %copy-done.53) | copy-start | bytes 1540
  1202.3 144.5 %copy-start.37 = (f32[128]{0:T(128)S(1)}, f32[128]{0:T(128)}, u32[]{:S(2)}) copy-start(f32[128]{0:T(128)} %copy-done.36) | copy-start | bytes 1540
  1202.3 144.8 %copy-start.45 = (f32[128]{0:T(128)S(1)}, f32[128]{0:T(128)}, u32[]{:S(2)}) copy-start(f32[128]{0:T(128)} %copy-done.43) | copy-start | bytes 1540
  1343.0 54.0 %copy-start.18 = (bf16[384,768]{1,0:T(8,128)(2,1)S(1)}, bf16[384,768]{1,0:T(8,128)(2,1)}, u32[]{:S(2)}) copy-start(bf16[384,768]{1,0:T(8,128)(2,1)} %reduce-scatter.10.cloned.1.call-done) | copy-start | bytes 1769476
  (24 other events, 70.4 us)
Sparse Core Ops, SparseCore 0:
  9.7 56.0 all-gather.15
  69.4 117.2 all-gather.17
  188.9 117.2 all-gather.19
  307.7 26.2 all-gather.21
  335.6 66.0 all-gather.23
  403.1 66.0 all-gather.25
  667.4 515.5 reduce-scatter.5
  1185.9 24.1 reduce-scatter.9
  1213.3 63.3 reduce-scatter.11
  1279.5 63.3 reduce-scatter.13
  1346.0 51.0 reduce-scatter.7
where the time goes:
time: 1740 us; the launch traced here: 1730 us
  waiting for transfers between devices  1050 us (60%)
  blocking collectives  391 us (22%)
  local copies, waits for them, and re-layouts  208 us (12%)
  matrix products  48 us (3%)
    reduce_scatter x1, waiting for transfers between devices, body(): lax.psum_scatter(key_terms.reshape(row_total, 2 * width), 'ctx', scatter_...  503 us
    psum x1, blocking collectives, body(): lax.psum((shards[0], shards[1], shards[2], shards[3], shards[4], shards[5...  330 us
    all_gather x1, waiting for transfers between devices, body(): value_span = lax.all_gather(values_local, 'ctx', axis=0, tiled=True)  103 us
    dynamic_update_slice x32, local copies, waits for them, and re-layouts, body(): lax.scan(back_step, zero_query, (key_blocks, value_blocks, jnp.arange(spa...  98.1 us
    unnamed x138, local copies, waits for them, and re-layouts  89.2 us
    all_gather x1, waiting for transfers between devices, body(): key_span = lax.all_gather(keys_local, 'ctx', axis=0, tiled=True)  79.1 us
    reduce_scatter x1, waiting for transfers between devices, body(): lax.psum_scatter(grad_fc_weight.astype(jnp.bfloat16), 'fsdp', scatter_dim...  66.5 us
    reduce_scatter x1, waiting for transfers between devices, body(): lax.psum_scatter(grad_out_weight.astype(jnp.bfloat16), 'fsdp', scatter_di...  66.2 us
  transfers between devices with their start and end apart: 11, of which 11 were waited for; matrix products, arithmetic and copies ran while one was open for 4% of the time, Pallas kernels for 0%

commit v1 on v0

--- a/solution.py
+++ b/solution.py
@@ -110,8 +110,12 @@
         jnp.zeros((head_count, row_count), jnp.float32),
         jnp.zeros((row_count, head_count, head_width), jnp.float32),
     )
-    key_span = lax.all_gather(keys_local, "ctx", axis=0, tiled=True)
-    value_span = lax.all_gather(values_local, "ctx", axis=0, tiled=True)
+    tokens_keep_up = lambda packet, original: jnp.split(
+        lax.all_gather(jnp.concatenate([packet, original], axis=1), "ctx", axis=0, tiled=True),
+        [packet.shape[1]],
+        axis=1,
+    )
+    key_span, value_span = tokens_keep_up(keys_local, values_local)
     span_total = key_span.shape[0]
     attend_span_rows = math.gcd(span_total, 512)
 

time: 1740 us -> 1830 us (1.052)
  local copies, waits for them, and re-layouts: 208 us -> 262 us
  waiting for transfers between devices: 1050 us -> 1080 us
    all_gather x2 -> x3, waiting for transfers between devices: 182 us -> 253 us  [the longest x1 101 us: body(): lax.all_gather(jnp.concatenate([packet, original], axis=1), 'ctx', axis=0...]
    all_gather x0 -> x2, local copies, waits for them, and re-layouts: none -> 32.4 us  [the longest x1 16.3 us: body(): lax.all_gather(keys_local, 'ctx', axis=0, tiled=True)]
    all_gather x1, waiting for transfers between devices: 65.6 us -> 39.4 us  [body(): lax.all_gather(w_fc, 'fsdp', axis=0, tiled=True)]
    unnamed x138 -> x132, local copies, waits for them, and re-layouts: 89.2 us -> 94 us
  transfers between devices with their start and end apart: 11 -> 12, of which waited for: 11 -> 11; matrix products, arithmetic and copies ran while one was open for 4% -> 10% of each run, Pallas kernels for 0% -> 0%
where the time goes in v1:
time: 1830 us
  waiting for transfers between devices  1080 us (59%)
  blocking collectives  392 us (21%)
  local copies, waits for them, and re-layouts  262 us (14%)
  matrix products  48 us (3%)
    reduce_scatter x1, waiting for transfers between devices, body(): lax.psum_scatter(key_terms.reshape(row_total, 2 * width), 'ctx', scatter_...  502 us
    psum x1, blocking collectives, body(): lax.psum((shards[0], shards[1], shards[2], shards[3], shards[4], shards[5...  330 us
    all_gather x1, waiting for transfers between devices, body(): lax.all_gather(jnp.concatenate([packet, original], axis=1), 'ctx', axis=0...  101 us
    dynamic_update_slice x32, local copies, waits for them, and re-layouts, body(): lax.scan(back_step, zero_query, (key_blocks, value_blocks, jnp.arange(spa...  98 us
    unnamed x132, local copies, waits for them, and re-layouts  94 us
    all_gather x1, waiting for transfers between devices, body(): lax.all_gather(keys_local, 'ctx', axis=0, tiled=True)  77.3 us
    all_gather x1, waiting for transfers between devices, body(): lax.all_gather(values_local, 'ctx', axis=0, tiled=True)  75.2 us
    reduce_scatter x1, waiting for transfers between devices, body(): lax.psum_scatter(grad_out_weight.astype(jnp.bfloat16), 'fsdp', scatter_di...  66.4 us
  transfers between devices with their start and end apart: 12, of which 11 were waited for; matrix products, arithmetic and copies ran while one was open for 10% of the time, Pallas kernels for 0%

profile of v1, /device:TPU:0, one launch (start us, length us, event | category | flops | bytes accessed | tf_op | source)
XLA Modules:
  0.0 1828.3 jit_solution(14699210527768904887)
XLA Ops:
  8.7 6.2 all-gather.1
  15.6 5.8 all-gather
  24.3 41.4 %all-gather.17.cloned.1.call-done = bf16[768,2304]{1,0:T(8,128)(2,1)} async-done(((bf16[384,2304]{1,0:T(8,128)(2,1)}), bf16[768,2304]{1,0:T(8,128)(2,1)}) %all-gather.17.cloned.1.call-update) | async-done | bytes 3538960 | tf_op jit(solution)/shard_map/all_gather | solution.py:67
  69.3 5.8 all-gather.3
  75.2 5.8 all-gather.2
  85.8 5.8 all-gather.4
  91.7 5.9 all-gather.7
  97.6 5.8 all-gather.6
  103.6 5.8 all-gather.5
  109.6 77.3 %all-gather.27.cloned.1.call-done = bf16[8192,768]{1,0:T(8,128)(2,1)} async-done(((bf16[128,768]{1,0:T(8,128)(2,1)}), bf16[8192,768]{1,0:T(8,128)(2,1)}) %all-gather.27.cloned.1.call-update) | async-done | bytes 12582928 | tf_op jit(solution)/shard_map/all_gather | solution.py:214
  186.9 16.3 copy.78
  203.1 9.4 copy.108
  212.6 18.6 %copy.81 = bf16[16,512,12,64]{1,3,2,0:T(8,128)(2,1)} copy(bf16[16,512,12,64]{1,0,3,2:T(8,128)(2,1)S(1)} %bitcast.172) | data formatting | bytes 25165824
  231.1 75.2 %all-gather.29.cloned.1.call-done = bf16[8192,768]{1,0:T(8,128)(2,1)} async-done(((bf16[128,768]{1,0:T(8,128)(2,1)}), bf16[8192,768]{1,0:T(8,128)(2,1)}) %all-gather.29.cloned.1.call-update) | async-done | bytes 12582928 | tf_op jit(solution)/shard_map/all_gather | solution.py:215
  306.3 16.2 copy.79
  322.5 9.6 copy.109
  332.1 18.6 %copy.82 = bf16[16,512,12,64]{1,3,2,0:T(8,128)(2,1)} copy(bf16[16,512,12,64]{1,0,3,2:T(8,128)(2,1)S(1)} %bitcast.174) | data formatting | bytes 25165824
  350.6 101.0 %all-gather.19.cloned.1.call-done = bf16[8192,1536]{1,0:T(8,128)(2,1)} async-done(((bf16[128,1536]{1,0:T(8,128)(2,1)}), bf16[8192,1536]{1,0:T(8,128)(2,1)}) %all-gather.19.cloned.1.call-update) | async-done | bytes 25165840 | tf_op jit(solution)/shard_map/all_gather | solution.py:114
  451.6 17.2 fusion.93
  468.8 15.8 copy.76
  484.6 16.3 copy.77
  500.9 5.9 while.34
  501.2 4.4 conditional.6
  509.0 39.4 %all-gather.23.cloned.1.call-done = bf16[768,3072]{1,0:T(8,128)(2,1)} async-done(((bf16[384,3072]{1,0:T(8,128)(2,1)}), bf16[768,3072]{1,0:T(8,128)(2,1)}) %all-gather.23.cloned.1.call-update) | async-done | bytes 4718608 | tf_op jit(solution)/shard_map/all_gather | solution.py:74
  551.7 64.4 %all-gather.25.cloned.1.call-done = bf16[3072,768]{1,0:T(8,128)(2,1)} async-done(((bf16[1536,768]{1,0:T(8,128)(2,1)}), bf16[3072,768]{1,0:T(8,128)(2,1)}) %all-gather.25.cloned.1.call-update) | async-done | bytes 4718608 | tf_op jit(solution)/shard_map/all_gather | solution.py:76
  616.1 5.4 fusion.96
  628.1 134.5 %while.35 = (s32[]{:T(128)}, f32[128,12,64]{0,2,1:T(8,128)}, f32[16,512,1536]{2,1,0:T(8,128)}, s32[16]{0:T(128)S(1)}, s32[]{:T(128)}, /*index=5*/bf16[16,512,12,...) while((s32[]{:T(128)}, f32[128,12,64]{0,2,1:T(8,128)}, ...), condition=%wide.region_16.17_spmd.clone, body=%wide.region_13.16_spmd.clone.sunk | while | flops 514491008 | bytes 40333600 | solution.py:263
  629.3 10.1 conditional.7
  649.5 3.8 constant_dynamic-update-slice_fusion.2
  657.3 3.8 constant_dynamic-update-slice_fusion.2
  680.7 3.7 constant_dynamic-update-slice_fusion.2
  688.5 3.8 constant_dynamic-update-slice_fusion.2
  696.3 3.7 constant_dynamic-update-slice_fusion.2
  704.1 3.8 constant_dynamic-update-slice_fusion.2
  711.9 3.8 constant_dynamic-update-slice_fusion.2
  727.5 3.8 constant_dynamic-update-slice_fusion.2
  743.1 3.8 constant_dynamic-update-slice_fusion.2
  750.9 3.9 constant_dynamic-update-slice_fusion.2
  770.5 3.8 convolution_convert_fusion
  775.8 501.6 %reduce-scatter.6.cloned.1.call-done = f32[128,1536]{1,0:T(8,128)} async-done(((f32[8192,1536]{1,0:T(8,128)}), f32[128,1536]{1,0:T(8,128)}) %reduce-scatter.6.cloned.1.call-update) | async-done | bytes 786448 | tf_op jit(solution)/shard_map/reduce_scatter | solution.py:266
  1283.0 6.1 all-gather.8
  1292.8 4.1 fusion.55
  1297.0 7.7 reduce-scatter.10.cloned.1.call-done
  1304.7 66.4 %reduce-scatter.12.cloned.1.call-done = bf16[384,3072]{1,0:T(8,128)(2,1)} async-done(((bf16[768,3072]{1,0:T(8,128)(2,1)}), bf16[384,3072]{1,0:T(8,128)(2,1)}) %reduce-scatter.12.cloned.1.call-update) | async-done | bytes 2359312 | tf_op jit(solution)/shard_map/reduce_scatter | solution.py:314
  1371.1 66.4 %reduce-scatter.14.cloned.1.call-done = bf16[1536,768]{1,0:T(8,128)(2,1)} async-done(((bf16[3072,768]{1,0:T(8,128)(2,1)}), bf16[1536,768]{1,0:T(8,128)(2,1)}) %reduce-scatter.14.cloned.1.call-update) | async-done | bytes 2359312 | tf_op jit(solution)/shard_map/reduce_scatter | solution.py:320
  1442.6 8.4 all-reduce.10
  1451.5 40.0 %reduce-scatter.8.cloned.1.call-done = bf16[384,2304]{1,0:T(8,128)(2,1)} async-done(((bf16[768,2304]{1,0:T(8,128)(2,1)}), bf16[384,2304]{1,0:T(8,128)(2,1)}) %reduce-scatter.8.cloned.1.call-update) | async-done | bytes 1769488 | tf_op jit(solution)/shard_map/reduce_scatter | solution.py:293
  1491.5 329.9 %all-reduce.12 = (f32[384]{0:T(512)}, f32[384]{0:T(512)}, f32[384,2304]{1,0:T(8,128)}, f32[384]{0:T(512)}, f32[384]{0:T(512)}, /*index=5*/f32[384,768]{1,0:T(8,1...) all-reduce(f32[384]{0:T(512)S(1)} %get-tuple-element.682, ...), channel_id=1, replica_groups=mesh['ctx'=64,'fsdp'=2] {'ctx'}, use_global_device_ids=true, to_apply=%region_22.23 | all-reduce | flops 3543552 | bytes 21270528 | tf_op jit(solution)/shard_map/psum | solution.py:327
  (380 shorter events, 144.3 us)
Async XLA Ops:
  7.2 58.5 %all-gather.17.cloned.1.call-start = ((), (), s32[]{:S(2)}) async-start(), calls=%async_computation.5 | async-start | bytes 5308416 | tf_op jit(solution)/shard_map/all_gather | solution.py:67
  7.9 61.4 %copy-start.47 = (bf16[384]{0:T(512)(128)(2,1)S(1)}, bf16[384]{0:T(512)(128)(2,1)}, u32[]{:S(2)}) copy-start(bf16[384]{0:T(512)(128)(2,1)} %param.28) | copy-start | bytes 2308
  7.9 67.3 %copy-start.48 = (bf16[384]{0:T(512)(128)(2,1)S(1)}, bf16[384]{0:T(512)(128)(2,1)}, u32[]{:S(2)}) copy-start(bf16[384]{0:T(512)(128)(2,1)} %param.29) | copy-start | bytes 2308
  7.9 178.9 %all-gather.27.cloned.1.call-start = ((), (), s32[]{:S(2)}) async-start(), calls=%async_computation.10 | async-start | bytes 12779520 | tf_op jit(solution)/shard_map/all_gather | solution.py:214
  14.9 66.2 %copy-start.26 = (f32[768]{0:T(1024)}, f32[768]{0:T(1024)S(1)}, u32[]{:S(2)}) copy-start(f32[768]{0:T(1024)S(1)} %reshape.253) | copy-start | bytes 9220
  21.5 59.6 %copy-start.19 = (f32[768]{0:T(1024)}, f32[768]{0:T(1024)S(1)}, u32[]{:S(2)}) copy-start(f32[768]{0:T(1024)S(1)} %reshape.252) | copy-start | bytes 9220
  22.6 58.5 %copy-start.31 = (f32[128]{0:T(128)}, f32[128]{0:T(128)S(1)}, u32[]{:S(2)}) copy-start(f32[128]{0:T(128)S(1)} %broadcast_multiply_fusion.1) | copy-start | bytes 1540
  24.3 56.8 %copy-start.36 = (f32[128]{0:T(128)}, f32[128]{0:T(128)S(1)}, u32[]{:S(2)}) copy-start(f32[128]{0:T(128)S(1)} %fusion.82) | copy-start | bytes 1540
  69.3 237.1 %all-gather.29.cloned.1.call-start = ((), (), s32[]{:S(2)}) async-start(), calls=%async_computation.11 | async-start | bytes 12779520 | tf_op jit(solution)/shard_map/all_gather | solution.py:215
  81.9 9.8 copy-start.46
  81.9 15.7 copy-start.50
  81.9 21.6 %copy-start.51 = (bf16[384]{0:T(512)(128)(2,1)S(1)}, bf16[384]{0:T(512)(128)(2,1)}, u32[]{:S(2)}) copy-start(bf16[384]{0:T(512)(128)(2,1)} %param.32) | copy-start | bytes 2308
  81.9 369.7 %all-gather.19.cloned.1.call-start = ((), (), s32[]{:S(2)}) async-start(), calls=%async_computation.6 | async-start | bytes 25559040 | tf_op jit(solution)/shard_map/all_gather | solution.py:114
  83.8 423.1 %all-gather.21.cloned.1.call-start = ((), (), s32[]{:S(2)}) async-start(), calls=%async_computation.7 | async-start | bytes 1769472 | tf_op jit(solution)/shard_map/all_gather | solution.py:70
  84.4 464.0 %all-gather.23.cloned.1.call-start = ((), (), s32[]{:S(2)}) async-start(), calls=%async_computation.8 | async-start | bytes 7077888 | tf_op jit(solution)/shard_map/all_gather | solution.py:74
  85.0 531.1 %all-gather.25.cloned.1.call-start = ((), (), s32[]{:S(2)}) async-start(), calls=%async_computation.9 | async-start | bytes 7077888 | tf_op jit(solution)/shard_map/all_gather | solution.py:76
  85.7 1191.7 %reduce-scatter.6.cloned.1.call-start = ((), (), s32[]{:S(2)}) async-start(), calls=%async_computation.12 | async-start | bytes 51118080 | tf_op jit(solution)/shard_map/reduce_scatter | solution.py:266
  103.5 444.9 %copy-start.24 = (f32[768]{0:T(1024)}, f32[768]{0:T(1024)S(1)}, u32[]{:S(2)}) copy-start(f32[768]{0:T(1024)S(1)} %reshape.258) | copy-start | bytes 9220
  109.4 439.0 %copy-start.21 = (f32[768]{0:T(1024)}, f32[768]{0:T(1024)S(1)}, u32[]{:S(2)}) copy-start(f32[768]{0:T(1024)S(1)} %reshape.257) | copy-start | bytes 9220
  500.9 6.0 copy-start.5
  506.9 119.3 %copy-start.11 = (bf16[128,12,64]{0,2,1:T(8,128)(2,1)}, bf16[128,12,64]{0,2,1:T(8,128)(2,1)S(1)}, u32[]{:S(2)}) copy-start(bf16[128,12,64]{0,2,1:T(8,128)(2,1)S(1)} %divide_convert_fusion) | copy-start | bytes 589828
  508.7 115.2 %copy-start.1 = (f32[128,768]{1,0:T(8,128)}, f32[128,768]{1,0:T(8,128)S(1)}, u32[]{:S(2)}) copy-start(f32[128,768]{1,0:T(8,128)S(1)} %get-tuple-element.670) | copy-start | bytes 1179652
  508.7 42.9 %copy-start.28 = (f32[128]{0:T(128)}, f32[128]{0:T(128)S(1)}, u32[]{:S(2)}) copy-start(f32[128]{0:T(128)S(1)} %broadcast_multiply_fusion) | copy-start | bytes 1540
  508.9 42.7 %copy-start.55 = (f32[128]{0:T(128)}, f32[128]{0:T(128)S(1)}, u32[]{:S(2)}) copy-start(f32[128]{0:T(128)S(1)} %multiply_reduce_fusion.2) | copy-start | bytes 1540
  509.0 42.7 %copy-start.33 = (f32[128]{0:T(128)}, f32[128]{0:T(128)S(1)}, u32[]{:S(2)}) copy-start(f32[128]{0:T(128)S(1)} %fusion.83) | copy-start | bytes 1540
  548.4 67.7 %copy-start.8 = (bf16[1,128,768]{2,1,0:T(8,128)(2,1)S(1)}, bf16[1,128,768]{2,1,0:T(8,128)(2,1)}, u32[]{:S(2)}) copy-start(bf16[1,128,768]{2,1,0:T(8,128)(2,1)} %param.24) | copy-start | bytes 589828
  551.7 69.9 %copy-start.3 = (f32[128,3072]{1,0:T(8,128)}, f32[128,3072]{1,0:T(8,128)S(1)}, u32[]{:S(2)}) copy-start(f32[128,3072]{1,0:T(8,128)S(1)} %convolution_add_fusion) | copy-start | bytes 4718596
  616.1 5.4 copy-start
  616.1 5.4 copy-start.22
  616.1 5.4 copy-start.29
  616.1 5.4 copy-start.34
  762.6 542.1 %reduce-scatter.10.cloned.1.call-start = ((), (), s32[]{:S(2)}) async-start(), calls=%async_computation.14 | async-start | bytes 1769472 | tf_op jit(solution)/shard_map/reduce_scatter | solution.py:302
  765.2 605.9 %reduce-scatter.12.cloned.1.call-start = ((), (), s32[]{:S(2)}) async-start(), calls=%async_computation.15 | async-start | bytes 7077888 | tf_op jit(solution)/shard_map/reduce_scatter | solution.py:314
  769.1 668.4 %reduce-scatter.14.cloned.1.call-start = ((), (), s32[]{:S(2)}) async-start(), calls=%async_computation.16 | async-start | bytes 7077888 | tf_op jit(solution)/shard_map/reduce_scatter | solution.py:320
  774.3 504.3 %copy-start.20 = (f32[768]{0:T(1024)S(1)}, f32[768]{0:T(1024)}, u32[]{:S(2)}) copy-start(f32[768]{0:T(1024)} %copy-done.19) | copy-start | bytes 9220
  774.3 504.3 %copy-start.27 = (f32[768]{0:T(1024)S(1)}, f32[768]{0:T(1024)}, u32[]{:S(2)}) copy-start(f32[768]{0:T(1024)} %copy-done.26) | copy-start | bytes 9220
  774.3 504.3 %copy-start.32 = (f32[128]{0:T(128)S(1)}, f32[128]{0:T(128)}, u32[]{:S(2)}) copy-start(f32[128]{0:T(128)} %copy-done.31) | copy-start | bytes 1540
  774.3 717.2 %reduce-scatter.8.cloned.1.call-start = ((), (), s32[]{:S(2)}) async-start(), calls=%async_computation.13 | async-start | bytes 5308416 | tf_op jit(solution)/shard_map/reduce_scatter | solution.py:293
  775.8 506.5 %copy-start.17 = (bf16[128,768]{1,0:T(8,128)(2,1)}, bf16[128,768]{1,0:T(8,128)(2,1)S(1)}, u32[]{:S(2)}) copy-start(bf16[128,768]{1,0:T(8,128)(2,1)S(1)} %copy.84) | copy-start | bytes 589828
  1282.3 8.0 copy-start.57
  1292.8 144.7 %copy-start.15 = (f32[128,1536]{1,0:T(8,128)S(1)}, f32[128,1536]{1,0:T(8,128)}, u32[]{:S(2)}) copy-start(f32[128,1536]{1,0:T(8,128)} %reduce-scatter.6.cloned.1.call-done) | copy-start | bytes 2359300
  1297.0 144.3 %copy-start.54 = (f32[128]{0:T(128)S(1)}, f32[128]{0:T(128)}, u32[]{:S(2)}) copy-start(f32[128]{0:T(128)} %copy-done.53) | copy-start | bytes 1540
  1297.0 144.3 %copy-start.37 = (f32[128]{0:T(128)S(1)}, f32[128]{0:T(128)}, u32[]{:S(2)}) copy-start(f32[128]{0:T(128)} %copy-done.36) | copy-start | bytes 1540
  1297.0 144.6 %copy-start.45 = (f32[128]{0:T(128)S(1)}, f32[128]{0:T(128)}, u32[]{:S(2)}) copy-start(f32[128]{0:T(128)} %copy-done.43) | copy-start | bytes 1540
  1437.5 5.1 copy-start.38
  1437.6 5.1 copy-start.39
  1437.6 5.1 copy-start.40
  1437.6 53.9 %copy-start.18 = (bf16[384,768]{1,0:T(8,128)(2,1)S(1)}, bf16[384,768]{1,0:T(8,128)(2,1)}, u32[]{:S(2)}) copy-start(bf16[384,768]{1,0:T(8,128)(2,1)} %reduce-scatter.10.cloned.1.call-done) | copy-start | bytes 1769476
  (22 other events, 56.7 us)
Sparse Core Ops, SparseCore 0:
  9.7 56.0 all-gather.16
  69.4 117.4 all-gather.26
  189.2 117.0 all-gather.28
  308.5 143.1 all-gather.18
  453.1 27.6 all-gather.20
  482.3 66.0 all-gather.22
  550.0 66.0 all-gather.24
  762.7 514.6 reduce-scatter.5
  1280.4 24.3 reduce-scatter.9
  1307.7 63.3 reduce-scatter.11
  1374.1 63.3 reduce-scatter.13
  1440.4 51.0 reduce-scatter.7
